TPU v7x, 256 devices: a whole 4x4x8 slice. The times are simulated.
256 devices in a mesh: gz: 64 (over x, z, core), gy: 4 (over y).
Axes of the slice: x: 4, y: 4, z: 8, core: 2. Of those that a mesh axis runs over, the one named last changes fastest.
Arguments:
- populations: float32 [19, 64, 128, 256], P(None, 'gz', 'gy'), may hold values from 0 to 0.5, as said below
- solid_fraction: float32 [64, 128, 256], P('gz', 'gy'), may hold values from 0 to 1
- labels: int32 [64, 128, 256], P('gz', 'gy'), may hold values from 0 to 4, as said below
Outputs:
- sensitivity: float32 [64, 128, 256], P('gz', 'gy')
- adjoint_populations: float32 [19, 64, 128, 256], P(None, 'gz', 'gy')
Inputs may be any that keep to these rules, and one draw needn't show every extreme that they name: `populations`: each population is w_q times a factor between 0.7 and 1.3. labels 3 appear only in the first plane along the feeding direction and 4 only in the last, in voxels that are not solid.
All inputs are finite; a program needn't handle non-finite values.
Results may differ from a plain program's by a relative error of at most 0.00028.
Values sent between devices are 32-bit elements; how exact they have to be, the bound alone decides.
A program may use at most 64 MiB of HBM per device.

v0:
```python
import jax
import jax.numpy as jnp
from jax import lax
from jax.sharding import PartitionSpec as P

STEPS = 2
OMEGA = 0.9
INLET_SPEED = 0.05


def padded_2(cells, sides, width):
    for axis, dim in sides:
        count = lax.axis_size(axis)
        head = lax.slice_in_dim(cells, 0, width, axis=dim)
        tail = lax.slice_in_dim(cells, cells.shape[dim] - width, cells.shape[dim], axis=dim)
        cells = jnp.concatenate(
            [
                lax.ppermute(tail, axis, [(i, (i + 1) % count) for i in range(count)]),
                cells,
                lax.ppermute(head, axis, [((i + 1) % count, i) for i in range(count)]),
            ],
            axis=dim,
        )
    return cells


def velocity_table():
    velocities = [(0, 0, 0)]
    for axis in range(3):
        for sign in (1, -1):
            vector = [0, 0, 0]
            vector[axis] = sign
            velocities.append(tuple(vector))
    for first in range(3):
        for second in range(first + 1, 3):
            for sign_a in (1, -1):
                for sign_b in (1, -1):
                    vector = [0, 0, 0]
                    vector[first] = sign_a
                    vector[second] = sign_b
                    velocities.append(tuple(vector))
    weights = [1.0 / 3.0] + [1.0 / 18.0] * 6 + [1.0 / 36.0] * 12
    opposite = [velocities.index(tuple((-e for e in vector))) for vector in velocities]
    return (velocities, weights, opposite)


def equilibrium(density, vel_x, vel_y, vel_z):
    velocities, weights, opposite = velocity_table()
    rows = []
    speed = vel_x * vel_x + vel_y * vel_y + vel_z * vel_z
    for index in range(19):
        cx, cy, cz = velocities[index]
        along = cx * vel_x + cy * vel_y + cz * vel_z
        rows.append(
            weights[index] * density * (1.0 + 3.0 * along + 4.5 * along * along - 1.5 * speed)
        )
    return jnp.stack(rows)


def moments(field):
    velocities, weights, opposite = velocity_table()
    density = jnp.sum(field, axis=0)
    mom_x = sum((velocities[q][0] * field[q] for q in range(19) if velocities[q][0] != 0))
    mom_y = sum((velocities[q][1] * field[q] for q in range(19) if velocities[q][1] != 0))
    mom_z = sum((velocities[q][2] * field[q] for q in range(19) if velocities[q][2] != 0))
    return (density, mom_x, mom_y, mom_z)


def collide(field, s_eff, labels):
    velocities, weights, opposite = velocity_table()
    density, mom_x, mom_y, mom_z = moments(field)
    feq = equilibrium(density, mom_x / density, mom_y / density, mom_z / density)
    rate = jnp.where(labels == 4, jnp.float32(1.0), jnp.float32(OMEGA))
    relaxed = field - rate * (field - feq)
    flipped = jnp.stack([field[opposite[q]] for q in range(19)])
    mixed = (1.0 - s_eff) * relaxed + s_eff * flipped
    ones = jnp.ones_like(density)
    inlet = equilibrium(ones, 0.0 * ones, 0.0 * ones, INLET_SPEED * ones)
    return jnp.where(labels == 3, inlet, mixed)


def energy(field, s_eff):
    density, mom_x, mom_y, mom_z = moments(field)
    return jnp.sum((1.0 - s_eff) * (mom_x * mom_x + mom_y * mom_y + mom_z * mom_z) / density)


def stream(field, sense):
    velocities, weights, opposite = velocity_table()
    depth = field.shape[1]
    height = field.shape[2]
    offsets = [(sense * v[0], sense * v[1], sense * v[2]) for v in velocities]
    padded = padded_2(field, (("gz", 1), ("gy", 2)), 1)
    moved = [
        padded[
            q,
            1 - offsets[q][2] : 1 - offsets[q][2] + depth,
            1 - offsets[q][1] : 1 - offsets[q][1] + height,
            :,
        ]
        for q in range(19)
    ]
    return jnp.stack([jnp.roll(moved[q], offsets[q][0], axis=2) for q in range(19)])


def global_energy(value):
    return lax.psum(value, ("gz", "gy"))


def on_device(populations, solid_fraction, labels):
    s_eff = jnp.where(
        labels == 1, solid_fraction, jnp.where(labels == 2, jnp.float32(1.0), jnp.float32(0.0))
    )
    states = [populations]
    total = jnp.float32(0.0)
    for step in range(STEPS):
        nxt = stream(collide(states[-1], s_eff, labels), 1)
        states.append(nxt)
        total = total + global_energy(energy(nxt, s_eff))
    energy_grad = jax.grad(energy, argnums=(0, 1))
    adjoint = jnp.zeros_like(populations)
    fraction_grad = jnp.zeros_like(solid_fraction)
    for step in reversed(range(STEPS)):
        grad_field, grad_frac = energy_grad(states[step + 1], s_eff)
        adjoint = adjoint + grad_field
        fraction_grad = fraction_grad + grad_frac
        pulled = stream(adjoint, -1)
        unused, pullback = jax.vjp(
            lambda field, frac: collide(field, frac, labels), states[step], s_eff
        )
        adjoint, grad_frac = pullback(pulled)
        fraction_grad = fraction_grad + grad_frac
    cells = (
        populations.shape[1]
        * populations.shape[2]
        * populations.shape[3]
        * lax.axis_size("gz")
        * lax.axis_size("gy")
    )
    mean_energy = total / (STEPS * cells)
    sensitivity = jnp.where(labels == 1, fraction_grad, jnp.float32(0.0)) / mean_energy
    return (sensitivity, adjoint / mean_energy)


def solution(mesh):
    in_specs = (P(None, "gz", "gy", None), P("gz", "gy", None), P("gz", "gy", None))
    out_specs = (P("gz", "gy", None), P(None, "gz", "gy", None))
    return jax.shard_map(
        on_device, mesh=mesh, in_specs=in_specs, out_specs=out_specs, check_vma=False
    )
```

profile of v0, /device:TPU:34, one launch (start us, length us, event | category | flops | bytes accessed | tf_op | source)
XLA Modules:
  0.0 174.0 jit_solution(15628574961668883643)
XLA Ops:
  1.5 1.1 reduce_sum.1999
  6.1 1.7 %collective-permute-start.1 = (f32[19,1,32,256]{3,2,1,0:T(8,128)S(1)}, f32[19,1,32,256]{3,2,1,0:T(8,128)S(1)}, u32[]{:S(2)}, u32[]{:S(2)}) collective-permute-start(f32[19,1,32,256]{3,2,1,0:T(8,128)S(1)} %add_select_fusion.1), channel_id=1, source_target_pairs={{4,0},{8,4},{12,8},{16,12},{20,16},{24,20},{28,24},{32,28},{36,32}... | collective-permute-start | bytes 1867784 | tf_op jit(solution)/shard_map/ppermute | solution.py:20
  8.1 7.6 %collective-permute-done.1 = f32[19,1,32,256]{3,2,1,0:T(8,128)S(1)} collective-permute-done((f32[19,1,32,256]{3,2,1,0:T(8,128)S(1)}, f32[19,1,32,256]{3,2,1,0:T(8,128)S(1)}, u32[]{:S(2)}, u32[]{:S(2)}) %collective-permute-start.1) | collective-permute-done | bytes 622624 | tf_op jit(solution)/shard_map/ppermute | solution.py:20
  15.9 1.7 collective-permute-start.2
  17.5 1.7 collective-permute-start.3
  19.3 2.1 %collective-permute-done.2 = f32[19,3,1,256]{3,2,1,0:T(1,128)S(1)} collective-permute-done((f32[19,3,1,256]{3,2,1,0:T(1,128)S(1)}, f32[19,3,1,256]{3,2,1,0:T(1,128)S(1)}, u32[]{:S(2)}, u32[]{:S(2)}) %collective-permute-start.2) | collective-permute-done | bytes 58400 | tf_op jit(solution)/shard_map/ppermute | solution.py:18
  26.1 1.0 collective-permute-start.5
  27.1 7.9 %collective-permute-done.4 = f32[19,1,32,256]{3,2,1,0:T(8,128)S(1)} collective-permute-done((f32[19,1,32,256]{3,2,1,0:T(8,128)S(1)}, f32[19,1,32,256]{3,2,1,0:T(8,128)S(1)}, u32[]{:S(2)}, u32[]{:S(2)}) %collective-permute-start.4) | collective-permute-done | bytes 622624 | tf_op jit(solution)/shard_map/ppermute | solution.py:18
  35.1 1.7 collective-permute-start.6
  36.7 1.7 collective-permute-start.7
  38.4 2.2 %collective-permute-done.6 = f32[19,3,1,256]{3,2,1,0:T(1,128)S(1)} collective-permute-done((f32[19,3,1,256]{3,2,1,0:T(1,128)S(1)}, f32[19,3,1,256]{3,2,1,0:T(1,128)S(1)}, u32[]{:S(2)}, u32[]{:S(2)}) %collective-permute-start.6) | collective-permute-done | bytes 58400 | tf_op jit(solution)/shard_map/ppermute | solution.py:18
  41.5 1.0 divide_reduce_fusion
  43.5 1.0 collective-permute-start.9
  44.7 7.7 %collective-permute-done.8 = f32[19,1,32,256]{3,2,1,0:T(8,128)S(1)} collective-permute-done((f32[19,1,32,256]{3,2,1,0:T(8,128)S(1)}, f32[19,1,32,256]{3,2,1,0:T(8,128)S(1)}, u32[]{:S(2)}, u32[]{:S(2)}) %collective-permute-start.8) | collective-permute-done | bytes 622624 | tf_op jit(solution)/shard_map/ppermute | solution.py:18
  52.5 3.1 %collective-permute-start.10 = (f32[19,3,1,256]{3,2,1,0:T(1,128)S(1)}, f32[19,3,1,256]{3,2,1,0:T(1,128)S(1)}, u32[]{:S(2)}, u32[]{:S(2)}) collective-permute-start(f32[19,3,1,256]{3,2,1,0:T(1,128)S(1)} %get-tuple-element.104), channel_id=1, source_target_pairs={{1,0},{2,1},{3,2},{0,3},{5,4},{6,5},{7,6},{4,7},{9,8},{10,9},{11,1... | collective-permute-start | bytes 175112 | tf_op jit(solution)/shard_map/ppermute | solution.py:20
  55.7 1.7 collective-permute-done.10
  57.5 3.6 %collective-permute-done.11 = f32[19,3,1,256]{3,2,1,0:T(1,128)S(1)} collective-permute-done((f32[19,3,1,256]{3,2,1,0:T(1,128)S(1)}, f32[19,3,1,256]{3,2,1,0:T(1,128)S(1)}, u32[]{:S(2)}, u32[]{:S(2)}) %collective-permute-start.11) | collective-permute-done | bytes 58400 | tf_op jit(solution)/shard_map/ppermute | solution.py:18
  65.1 1.4 collective-permute-start.12
  68.2 88.7 %psum.16 = f32[]{:T(128)} all-reduce(f32[]{:T(128)S(6)} %add.7467), channel_id=1, replica_groups=mesh['gz'=64,'gy'=4] {'gz','gy'}, use_global_device_ids=true, to_apply=%region_6.7 | all-reduce | flops 1 | bytes 8 | tf_op jit(solution)/shard_map/psum | solution.py:106
  157.9 3.0 %collective-permute-start.14 = (f32[19,3,1,256]{3,2,1,0:T(1,128)S(1)}, f32[19,3,1,256]{3,2,1,0:T(1,128)S(1)}, u32[]{:S(2)}, u32[]{:S(2)}) collective-permute-start(f32[19,3,1,256]{3,2,1,0:T(1,128)S(1)} %get-tuple-element.102), channel_id=1, source_target_pairs={{1,0},{2,1},{3,2},{0,3},{5,4},{6,5},{7,6},{4,7},{9,8},{10,9},{11,1... | collective-permute-start | bytes 175112 | tf_op jit(solution)/shard_map/ppermute | solution.py:20
  161.0 1.7 collective-permute-done.14
  162.8 3.6 %collective-permute-done.15 = f32[19,3,1,256]{3,2,1,0:T(1,128)S(1)} collective-permute-done((f32[19,3,1,256]{3,2,1,0:T(1,128)S(1)}, f32[19,3,1,256]{3,2,1,0:T(1,128)S(1)}, u32[]{:S(2)}, u32[]{:S(2)}) %collective-permute-start.15) | collective-permute-done | bytes 58400 | tf_op jit(solution)/shard_map/ppermute | solution.py:18
  167.7 1.0 copy-done.8
  172.9 1.1 add_divide_fusion
  (277 shorter events, 21.6 us)
Async XLA Ops:
  0.6 2.0 %copy-start = (f32[19,1,32,256]{3,2,1,0:T(8,128)S(1)}, f32[19,1,32,256]{3,2,1,0:T(8,128)}, u32[]{:S(2)}) copy-start(f32[19,1,32,256]{3,2,1,0:T(8,128)} %param.3) | copy-start | bytes 1867780
  6.1 9.7 %collective-permute-start = (f32[19,1,32,256]{3,2,1,0:T(8,128)S(1)}, f32[19,1,32,256]{3,2,1,0:T(8,128)S(1)}, u32[]{:S(2)}, u32[]{:S(2)}) collective-permute-start(f32[19,1,32,256]{3,2,1,0:T(8,128)S(1)} %add_select_fusion.1), channel_id=1, source_target_pairs={{0,4},{4,8},{8,12},{12,16},{16,20},{20,24},{24,28},{28,32},{32,36}... | collective-permute-start | bytes 1867784 | tf_op jit(solution)/shard_map/ppermute | solution.py:18
  6.1 9.5 %collective-permute-start.1 = (f32[19,1,32,256]{3,2,1,0:T(8,128)S(1)}, f32[19,1,32,256]{3,2,1,0:T(8,128)S(1)}, u32[]{:S(2)}, u32[]{:S(2)}) collective-permute-start(f32[19,1,32,256]{3,2,1,0:T(8,128)S(1)} %add_select_fusion.1), channel_id=1, source_target_pairs={{4,0},{8,4},{12,8},{16,12},{20,16},{24,20},{28,24},{32,28},{36,32}... | collective-permute-start | bytes 1867784 | tf_op jit(solution)/shard_map/ppermute | solution.py:20
  15.9 5.5 %collective-permute-start.2 = (f32[19,3,1,256]{3,2,1,0:T(1,128)S(1)}, f32[19,3,1,256]{3,2,1,0:T(1,128)S(1)}, u32[]{:S(2)}, u32[]{:S(2)}) collective-permute-start(f32[19,3,1,256]{3,2,1,0:T(1,128)S(1)} %get-tuple-element.111), channel_id=1, source_target_pairs={{0,1},{1,2},{2,3},{3,0},{4,5},{5,6},{6,7},{7,4},{8,9},{9,10},{10,1... | collective-permute-start | bytes 175112 | tf_op jit(solution)/shard_map/ppermute | solution.py:18
  17.5 4.2 %collective-permute-start.3 = (f32[19,3,1,256]{3,2,1,0:T(1,128)S(1)}, f32[19,3,1,256]{3,2,1,0:T(1,128)S(1)}, u32[]{:S(2)}, u32[]{:S(2)}) collective-permute-start(f32[19,3,1,256]{3,2,1,0:T(1,128)S(1)} %get-tuple-element.112), channel_id=1, source_target_pairs={{1,0},{2,1},{3,2},{0,3},{5,4},{6,5},{7,6},{4,7},{9,8},{10,9},{11,1... | collective-permute-start | bytes 175112 | tf_op jit(solution)/shard_map/ppermute | solution.py:20
  23.0 1.5 copy-start.5
  25.3 9.7 %collective-permute-start.4 = (f32[19,1,32,256]{3,2,1,0:T(8,128)S(1)}, f32[19,1,32,256]{3,2,1,0:T(8,128)S(1)}, u32[]{:S(2)}, u32[]{:S(2)}) collective-permute-start(f32[19,1,32,256]{3,2,1,0:T(8,128)S(1)} %add_select_fusion), channel_id=1, source_target_pairs={{0,4},{4,8},{8,12},{12,16},{16,20},{20,24},{24,28},{28,32},{32,36}... | collective-permute-start | bytes 1867784 | tf_op jit(solution)/shard_map/ppermute | solution.py:18
  26.1 8.9 %collective-permute-start.5 = (f32[19,1,32,256]{3,2,1,0:T(8,128)S(1)}, f32[19,1,32,256]{3,2,1,0:T(8,128)S(1)}, u32[]{:S(2)}, u32[]{:S(2)}) collective-permute-start(f32[19,1,32,256]{3,2,1,0:T(8,128)S(1)} %add_select_fusion), channel_id=1, source_target_pairs={{4,0},{8,4},{12,8},{16,12},{20,16},{24,20},{28,24},{32,28},{36,32}... | collective-permute-start | bytes 1867784 | tf_op jit(solution)/shard_map/ppermute | solution.py:20
  35.1 5.5 %collective-permute-start.6 = (f32[19,3,1,256]{3,2,1,0:T(1,128)S(1)}, f32[19,3,1,256]{3,2,1,0:T(1,128)S(1)}, u32[]{:S(2)}, u32[]{:S(2)}) collective-permute-start(f32[19,3,1,256]{3,2,1,0:T(1,128)S(1)} %get-tuple-element.107), channel_id=1, source_target_pairs={{0,1},{1,2},{2,3},{3,0},{4,5},{5,6},{6,7},{7,4},{8,9},{9,10},{10,1... | collective-permute-start | bytes 175112 | tf_op jit(solution)/shard_map/ppermute | solution.py:18
  36.7 4.2 %collective-permute-start.7 = (f32[19,3,1,256]{3,2,1,0:T(1,128)S(1)}, f32[19,3,1,256]{3,2,1,0:T(1,128)S(1)}, u32[]{:S(2)}, u32[]{:S(2)}) collective-permute-start(f32[19,3,1,256]{3,2,1,0:T(1,128)S(1)} %get-tuple-element.108), channel_id=1, source_target_pairs={{1,0},{2,1},{3,2},{0,3},{5,4},{6,5},{7,6},{4,7},{9,8},{10,9},{11,1... | collective-permute-start | bytes 175112 | tf_op jit(solution)/shard_map/ppermute | solution.py:20
  42.6 9.7 %collective-permute-start.8 = (f32[19,1,32,256]{3,2,1,0:T(8,128)S(1)}, f32[19,1,32,256]{3,2,1,0:T(8,128)S(1)}, u32[]{:S(2)}, u32[]{:S(2)}) collective-permute-start(f32[19,1,32,256]{3,2,1,0:T(8,128)S(1)} %add_add_fusion.1), channel_id=1, source_target_pairs={{0,4},{4,8},{8,12},{12,16},{16,20},{20,24},{24,28},{28,32},{32,36}... | collective-permute-start | bytes 1867784 | tf_op jit(solution)/shard_map/ppermute | solution.py:18
  43.5 8.9 %collective-permute-start.9 = (f32[19,1,32,256]{3,2,1,0:T(8,128)S(1)}, f32[19,1,32,256]{3,2,1,0:T(8,128)S(1)}, u32[]{:S(2)}, u32[]{:S(2)}) collective-permute-start(f32[19,1,32,256]{3,2,1,0:T(8,128)S(1)} %add_add_fusion.1), channel_id=1, source_target_pairs={{4,0},{8,4},{12,8},{16,12},{20,16},{24,20},{28,24},{32,28},{36,32}... | collective-permute-start | bytes 1867784 | tf_op jit(solution)/shard_map/ppermute | solution.py:20
  52.5 5.0 %collective-permute-start.10 = (f32[19,3,1,256]{3,2,1,0:T(1,128)S(1)}, f32[19,3,1,256]{3,2,1,0:T(1,128)S(1)}, u32[]{:S(2)}, u32[]{:S(2)}) collective-permute-start(f32[19,3,1,256]{3,2,1,0:T(1,128)S(1)} %get-tuple-element.104), channel_id=1, source_target_pairs={{1,0},{2,1},{3,2},{0,3},{5,4},{6,5},{7,6},{4,7},{9,8},{10,9},{11,1... | collective-permute-start | bytes 175112 | tf_op jit(solution)/shard_map/ppermute | solution.py:20
  55.7 5.4 %collective-permute-start.11 = (f32[19,3,1,256]{3,2,1,0:T(1,128)S(1)}, f32[19,3,1,256]{3,2,1,0:T(1,128)S(1)}, u32[]{:S(2)}, u32[]{:S(2)}) collective-permute-start(f32[19,3,1,256]{3,2,1,0:T(1,128)S(1)} %get-tuple-element.103), channel_id=1, source_target_pairs={{0,1},{1,2},{2,3},{3,0},{4,5},{5,6},{6,7},{7,4},{8,9},{9,10},{10,1... | collective-permute-start | bytes 175112 | tf_op jit(solution)/shard_map/ppermute | solution.py:18
  62.3 1.8 %copy-start.1 = (f32[19,1,32,256]{3,2,1,0:T(8,128)}, f32[19,1,32,256]{3,2,1,0:T(8,128)S(1)}, u32[]{:S(2)}) copy-start(f32[19,1,32,256]{3,2,1,0:T(8,128)S(1)} %constant_dynamic-update-slice_fusion.108) | copy-start | bytes 1867780
  65.1 92.7 %collective-permute-start.12 = (f32[19,1,32,256]{3,2,1,0:T(8,128)S(1)}, f32[19,1,32,256]{3,2,1,0:T(8,128)S(1)}, u32[]{:S(2)}, u32[]{:S(2)}) collective-permute-start(f32[19,1,32,256]{3,2,1,0:T(8,128)S(1)} %add_add_fusion), channel_id=1, source_target_pairs={{0,4},{4,8},{8,12},{12,16},{16,20},{20,24},{24,28},{28,32},{32,36}... | collective-permute-start | bytes 1867784 | tf_op jit(solution)/shard_map/ppermute | solution.py:18
  66.5 91.3 %collective-permute-start.13 = (f32[19,1,32,256]{3,2,1,0:T(8,128)S(1)}, f32[19,1,32,256]{3,2,1,0:T(8,128)S(1)}, u32[]{:S(2)}, u32[]{:S(2)}) collective-permute-start(f32[19,1,32,256]{3,2,1,0:T(8,128)S(1)} %add_add_fusion), channel_id=1, source_target_pairs={{4,0},{8,4},{12,8},{16,12},{20,16},{24,20},{28,24},{32,28},{36,32}... | collective-permute-start | bytes 1867784 | tf_op jit(solution)/shard_map/ppermute | solution.py:20
  157.9 4.9 %collective-permute-start.14 = (f32[19,3,1,256]{3,2,1,0:T(1,128)S(1)}, f32[19,3,1,256]{3,2,1,0:T(1,128)S(1)}, u32[]{:S(2)}, u32[]{:S(2)}) collective-permute-start(f32[19,3,1,256]{3,2,1,0:T(1,128)S(1)} %get-tuple-element.102), channel_id=1, source_target_pairs={{1,0},{2,1},{3,2},{0,3},{5,4},{6,5},{7,6},{4,7},{9,8},{10,9},{11,1... | collective-permute-start | bytes 175112 | tf_op jit(solution)/shard_map/ppermute | solution.py:20
  161.0 5.4 %collective-permute-start.15 = (f32[19,3,1,256]{3,2,1,0:T(1,128)S(1)}, f32[19,3,1,256]{3,2,1,0:T(1,128)S(1)}, u32[]{:S(2)}, u32[]{:S(2)}) collective-permute-start(f32[19,3,1,256]{3,2,1,0:T(1,128)S(1)} %get-tuple-element.101), channel_id=1, source_target_pairs={{0,1},{1,2},{2,3},{3,0},{4,5},{5,6},{6,7},{7,4},{8,9},{9,10},{10,1... | collective-permute-start | bytes 175112 | tf_op jit(solution)/shard_map/ppermute | solution.py:18
  167.6 1.1 copy-start.8
  167.6 1.3 copy-start.10
  167.7 1.4 copy-start.2
  167.7 1.6 copy-start.4
  167.7 1.8 %copy-start.6 = (f32[19,1,32,256]{3,2,1,0:T(8,128)S(1)}, f32[19,1,32,256]{3,2,1,0:T(8,128)}, u32[]{:S(2)}) copy-start(f32[19,1,32,256]{3,2,1,0:T(8,128)} %copy-done.5) | copy-start | bytes 1867780
  (7 other events, 5.6 us)
where the time goes:
time: 174 us
  blocking collectives  88.7 us (51%)
  waiting for transfers between devices  38.5 us (22%)
  starting transfers between devices  20 us (11%)
  other arithmetic  13.8 us (8%)
  local copies, waits for them, and re-layouts  9.47 us (5%)
  between operations  3.68 us (2%)
    psum x1, blocking collectives, global_energy(): return lax.psum(value, ('gz', 'gy'))  88.7 us
    ppermute x8, waiting for transfers between devices, padded_2(): lax.ppermute(tail, axis, [(i, (i + 1) % count) for i in range(count)])  27 us
    ppermute x8, starting transfers between devices, padded_2(): lax.ppermute(head, axis, [((i + 1) % count, i) for i in range(count)])  13.7 us
    ppermute x8, waiting for transfers between devices, padded_2(): lax.ppermute(head, axis, [((i + 1) % count, i) for i in range(count)])  11.5 us
    ppermute x8, starting transfers between devices, padded_2(): lax.ppermute(tail, axis, [(i, (i + 1) % count) for i in range(count)])  6.31 us
    unnamed x76, local copies, waits for them, and re-layouts  6.28 us
    unnamed x79, other arithmetic  4.62 us
  transfers between devices with their start and end apart: 16, of which 12 were waited for; matrix products, arithmetic and copies ran while one was open for 1% of the time, Pallas kernels for 0%

commit v1 on v0

--- a/solution.py
+++ b/solution.py
@@ -103,7 +103,7 @@
 
 
 def global_energy(value):
-    return lax.psum(value, ("gz", "gy"))
+    return jax.lax.psum(jax.lax.psum(value, "gy"), "gz")
 
 
 def on_device(populations, solid_fraction, labels):

time: 174 us -> 233 us (1.34)
  the two profiles are of different devices: /device:TPU:34 before, /device:TPU:1 now
where the time goes in v1:
time: 233 us; the launch traced here: 232 us
  blocking collectives  137 us (59%)
  starting transfers between devices  39.7 us (17%)
  waiting for transfers between devices  28.6 us (12%)
  other arithmetic  13.8 us (6%)
  local copies, waits for them, and re-layouts  9.46 us (4%)
  between operations  3.66 us (2%)
    psum x2, blocking collectives, global_energy(): return jax.lax.psum(jax.lax.psum(value, 'gy'), 'gz')  137 us
    ppermute x8, starting transfers between devices, padded_2(): lax.ppermute(head, axis, [((i + 1) % count, i) for i in range(count)])  30.6 us
    ppermute x8, waiting for transfers between devices, padded_2(): lax.ppermute(head, axis, [((i + 1) % count, i) for i in range(count)])  15.3 us
    ppermute x8, waiting for transfers between devices, padded_2(): lax.ppermute(tail, axis, [(i, (i + 1) % count) for i in range(count)])  13.4 us
    ppermute x8, starting transfers between devices, padded_2(): lax.ppermute(tail, axis, [(i, (i + 1) % count) for i in range(count)])  9.08 us
    unnamed x76, local copies, waits for them, and re-layouts  6.27 us
  transfers between devices with their start and end apart: 16, of which 11 were waited for; matrix products, arithmetic and copies ran while one was open for 1% of the time, Pallas kernels for 0%

profile of v1, /device:TPU:1, one launch (start us, length us, event | category | flops | bytes accessed | tf_op | source)
XLA Modules:
  0.0 232.4 jit_solution(702206534442771621)
XLA Ops:
  6.1 3.0 %collective-permute-start = (f32[19,1,32,256]{3,2,1,0:T(8,128)S(1)}, f32[19,1,32,256]{3,2,1,0:T(8,128)S(1)}, u32[]{:S(2)}, u32[]{:S(2)}) collective-permute-start(f32[19,1,32,256]{3,2,1,0:T(8,128)S(1)} %add_select_fusion.1), channel_id=1, source_target_pairs={{0,4},{4,8},{8,12},{12,16},{16,20},{20,24},{24,28},{28,32},{32,36}... | collective-permute-start | bytes 1867784 | tf_op jit(solution)/shard_map/ppermute | solution.py:18
  9.5 9.6 %collective-permute-done.1 = f32[19,1,32,256]{3,2,1,0:T(8,128)S(1)} collective-permute-done((f32[19,1,32,256]{3,2,1,0:T(8,128)S(1)}, f32[19,1,32,256]{3,2,1,0:T(8,128)S(1)}, u32[]{:S(2)}, u32[]{:S(2)}) %collective-permute-start.1) | collective-permute-done | bytes 622624 | tf_op jit(solution)/shard_map/ppermute | solution.py:20
  19.3 1.4 collective-permute-start.2
  20.7 1.5 collective-permute-start.3
  22.3 1.4 collective-permute-done.2
  28.3 4.2 %collective-permute-start.5 = (f32[19,1,32,256]{3,2,1,0:T(8,128)S(1)}, f32[19,1,32,256]{3,2,1,0:T(8,128)S(1)}, u32[]{:S(2)}, u32[]{:S(2)}) collective-permute-start(f32[19,1,32,256]{3,2,1,0:T(8,128)S(1)} %add_select_fusion), channel_id=1, source_target_pairs={{4,0},{8,4},{12,8},{16,12},{20,16},{24,20},{28,24},{32,28},{36,32}... | collective-permute-start | bytes 1867784 | tf_op jit(solution)/shard_map/ppermute | solution.py:20
  32.6 3.0 %collective-permute-done.4 = f32[19,1,32,256]{3,2,1,0:T(8,128)S(1)} collective-permute-done((f32[19,1,32,256]{3,2,1,0:T(8,128)S(1)}, f32[19,1,32,256]{3,2,1,0:T(8,128)S(1)}, u32[]{:S(2)}, u32[]{:S(2)}) %collective-permute-start.4) | collective-permute-done | bytes 622624 | tf_op jit(solution)/shard_map/ppermute | solution.py:18
  35.5 2.5 %collective-permute-done.5 = f32[19,1,32,256]{3,2,1,0:T(8,128)S(1)} collective-permute-done((f32[19,1,32,256]{3,2,1,0:T(8,128)S(1)}, f32[19,1,32,256]{3,2,1,0:T(8,128)S(1)}, u32[]{:S(2)}, u32[]{:S(2)}) %collective-permute-start.5) | collective-permute-done | bytes 622624 | tf_op jit(solution)/shard_map/ppermute | solution.py:20
  38.1 1.4 collective-permute-start.6
  39.5 1.4 collective-permute-start.7
  40.9 1.9 collective-permute-done.6
  45.7 7.6 %collective-permute-start.9 = (f32[19,1,32,256]{3,2,1,0:T(8,128)S(1)}, f32[19,1,32,256]{3,2,1,0:T(8,128)S(1)}, u32[]{:S(2)}, u32[]{:S(2)}) collective-permute-start(f32[19,1,32,256]{3,2,1,0:T(8,128)S(1)} %add_add_fusion.1), channel_id=1, source_target_pairs={{4,0},{8,4},{12,8},{16,12},{20,16},{24,20},{28,24},{32,28},{36,32}... | collective-permute-start | bytes 1867784 | tf_op jit(solution)/shard_map/ppermute | solution.py:20
  53.6 1.2 collective-permute-done.8
  55.5 2.8 %collective-permute-start.10 = (f32[19,3,1,256]{3,2,1,0:T(1,128)S(1)}, f32[19,3,1,256]{3,2,1,0:T(1,128)S(1)}, u32[]{:S(2)}, u32[]{:S(2)}) collective-permute-start(f32[19,3,1,256]{3,2,1,0:T(1,128)S(1)} %get-tuple-element.104), channel_id=1, source_target_pairs={{1,0},{2,1},{3,2},{0,3},{5,4},{6,5},{7,6},{4,7},{9,8},{10,9},{11,1... | collective-permute-start | bytes 175112 | tf_op jit(solution)/shard_map/ppermute | solution.py:20
  58.4 1.2 collective-permute-done.10
  59.7 3.3 %collective-permute-done.11 = f32[19,3,1,256]{3,2,1,0:T(1,128)S(1)} collective-permute-done((f32[19,3,1,256]{3,2,1,0:T(1,128)S(1)}, f32[19,3,1,256]{3,2,1,0:T(1,128)S(1)}, u32[]{:S(2)}, u32[]{:S(2)}) %collective-permute-start.11) | collective-permute-done | bytes 58400 | tf_op jit(solution)/shard_map/ppermute | solution.py:18
  67.0 1.2 collective-permute-start.12
  68.2 11.0 %collective-permute-start.13 = (f32[19,1,32,256]{3,2,1,0:T(8,128)S(1)}, f32[19,1,32,256]{3,2,1,0:T(8,128)S(1)}, u32[]{:S(2)}, u32[]{:S(2)}) collective-permute-start(f32[19,1,32,256]{3,2,1,0:T(8,128)S(1)} %add_add_fusion), channel_id=1, source_target_pairs={{4,0},{8,4},{12,8},{16,12},{20,16},{24,20},{28,24},{32,28},{36,32}... | collective-permute-start | bytes 1867784 | tf_op jit(solution)/shard_map/ppermute | solution.py:20
  80.4 7.2 %psum.33 = f32[]{:T(128)} all-reduce(f32[]{:T(128)S(6)} %add.7471), channel_id=1, replica_groups=mesh['gz'=64,'gy'=4] {'gy'}, use_global_device_ids=true, to_apply=%region_6.7 | all-reduce | flops 1 | bytes 8 | tf_op jit(solution)/shard_map/psum | solution.py:106
  87.6 130.1 %psum.32 = f32[]{:T(128)} all-reduce(f32[]{:T(128)} %psum.33), channel_id=1, replica_groups=mesh['gz'=64,'gy'=4] {'gz'}, use_global_device_ids=true, to_apply=%region_7.8 | all-reduce | flops 1 | bytes 8 | tf_op jit(solution)/shard_map/psum | solution.py:106
  218.7 1.8 collective-permute-start.14
  220.6 1.5 collective-permute-done.14
  222.1 2.7 %collective-permute-done.15 = f32[19,3,1,256]{3,2,1,0:T(1,128)S(1)} collective-permute-done((f32[19,3,1,256]{3,2,1,0:T(1,128)S(1)}, f32[19,3,1,256]{3,2,1,0:T(1,128)S(1)}, u32[]{:S(2)}, u32[]{:S(2)}) %collective-permute-start.15) | collective-permute-done | bytes 58400 | tf_op jit(solution)/shard_map/ppermute | solution.py:18
  231.3 1.1 add_divide_fusion
  (278 shorter events, 25.0 us)
Async XLA Ops:
  0.6 2.0 copy-start
  6.1 13.1 %collective-permute-start = (f32[19,1,32,256]{3,2,1,0:T(8,128)S(1)}, f32[19,1,32,256]{3,2,1,0:T(8,128)S(1)}, u32[]{:S(2)}, u32[]{:S(2)}) collective-permute-start(f32[19,1,32,256]{3,2,1,0:T(8,128)S(1)} %add_select_fusion.1), channel_id=1, source_target_pairs={{0,4},{4,8},{8,12},{12,16},{16,20},{20,24},{24,28},{28,32},{32,36}... | collective-permute-start | bytes 1867784 | tf_op jit(solution)/shard_map/ppermute | solution.py:18
  9.1 10.0 %collective-permute-start.1 = (f32[19,1,32,256]{3,2,1,0:T(8,128)S(1)}, f32[19,1,32,256]{3,2,1,0:T(8,128)S(1)}, u32[]{:S(2)}, u32[]{:S(2)}) collective-permute-start(f32[19,1,32,256]{3,2,1,0:T(8,128)S(1)} %add_select_fusion.1), channel_id=1, source_target_pairs={{4,0},{8,4},{12,8},{16,12},{20,16},{24,20},{28,24},{32,28},{36,32}... | collective-permute-start | bytes 1867784 | tf_op jit(solution)/shard_map/ppermute | solution.py:20
  19.3 4.4 %collective-permute-start.2 = (f32[19,3,1,256]{3,2,1,0:T(1,128)S(1)}, f32[19,3,1,256]{3,2,1,0:T(1,128)S(1)}, u32[]{:S(2)}, u32[]{:S(2)}) collective-permute-start(f32[19,3,1,256]{3,2,1,0:T(1,128)S(1)} %get-tuple-element.111), channel_id=1, source_target_pairs={{0,1},{1,2},{2,3},{3,0},{4,5},{5,6},{6,7},{7,4},{8,9},{9,10},{10,1... | collective-permute-start | bytes 175112 | tf_op jit(solution)/shard_map/ppermute | solution.py:18
  20.7 3.0 %collective-permute-start.3 = (f32[19,3,1,256]{3,2,1,0:T(1,128)S(1)}, f32[19,3,1,256]{3,2,1,0:T(1,128)S(1)}, u32[]{:S(2)}, u32[]{:S(2)}) collective-permute-start(f32[19,3,1,256]{3,2,1,0:T(1,128)S(1)} %get-tuple-element.112), channel_id=1, source_target_pairs={{1,0},{2,1},{3,2},{0,3},{5,4},{6,5},{7,6},{4,7},{9,8},{10,9},{11,1... | collective-permute-start | bytes 175112 | tf_op jit(solution)/shard_map/ppermute | solution.py:20
  25.0 1.5 copy-start.5
  27.3 8.2 %collective-permute-start.4 = (f32[19,1,32,256]{3,2,1,0:T(8,128)S(1)}, f32[19,1,32,256]{3,2,1,0:T(8,128)S(1)}, u32[]{:S(2)}, u32[]{:S(2)}) collective-permute-start(f32[19,1,32,256]{3,2,1,0:T(8,128)S(1)} %add_select_fusion), channel_id=1, source_target_pairs={{0,4},{4,8},{8,12},{12,16},{16,20},{20,24},{24,28},{28,32},{32,36}... | collective-permute-start | bytes 1867784 | tf_op jit(solution)/shard_map/ppermute | solution.py:18
  28.3 9.7 %collective-permute-start.5 = (f32[19,1,32,256]{3,2,1,0:T(8,128)S(1)}, f32[19,1,32,256]{3,2,1,0:T(8,128)S(1)}, u32[]{:S(2)}, u32[]{:S(2)}) collective-permute-start(f32[19,1,32,256]{3,2,1,0:T(8,128)S(1)} %add_select_fusion), channel_id=1, source_target_pairs={{4,0},{8,4},{12,8},{16,12},{20,16},{24,20},{28,24},{32,28},{36,32}... | collective-permute-start | bytes 1867784 | tf_op jit(solution)/shard_map/ppermute | solution.py:20
  38.1 4.6 %collective-permute-start.6 = (f32[19,3,1,256]{3,2,1,0:T(1,128)S(1)}, f32[19,3,1,256]{3,2,1,0:T(1,128)S(1)}, u32[]{:S(2)}, u32[]{:S(2)}) collective-permute-start(f32[19,3,1,256]{3,2,1,0:T(1,128)S(1)} %get-tuple-element.107), channel_id=1, source_target_pairs={{0,1},{1,2},{2,3},{3,0},{4,5},{5,6},{6,7},{7,4},{8,9},{9,10},{10,1... | collective-permute-start | bytes 175112 | tf_op jit(solution)/shard_map/ppermute | solution.py:18
  39.5 3.5 %collective-permute-start.7 = (f32[19,3,1,256]{3,2,1,0:T(1,128)S(1)}, f32[19,3,1,256]{3,2,1,0:T(1,128)S(1)}, u32[]{:S(2)}, u32[]{:S(2)}) collective-permute-start(f32[19,3,1,256]{3,2,1,0:T(1,128)S(1)} %get-tuple-element.108), channel_id=1, source_target_pairs={{1,0},{2,1},{3,2},{0,3},{5,4},{6,5},{7,6},{4,7},{9,8},{10,9},{11,1... | collective-permute-start | bytes 175112 | tf_op jit(solution)/shard_map/ppermute | solution.py:20
  44.7 10.1 %collective-permute-start.8 = (f32[19,1,32,256]{3,2,1,0:T(8,128)S(1)}, f32[19,1,32,256]{3,2,1,0:T(8,128)S(1)}, u32[]{:S(2)}, u32[]{:S(2)}) collective-permute-start(f32[19,1,32,256]{3,2,1,0:T(8,128)S(1)} %add_add_fusion.1), channel_id=1, source_target_pairs={{0,4},{4,8},{8,12},{12,16},{16,20},{20,24},{24,28},{28,32},{32,36}... | collective-permute-start | bytes 1867784 | tf_op jit(solution)/shard_map/ppermute | solution.py:18
  45.7 9.7 %collective-permute-start.9 = (f32[19,1,32,256]{3,2,1,0:T(8,128)S(1)}, f32[19,1,32,256]{3,2,1,0:T(8,128)S(1)}, u32[]{:S(2)}, u32[]{:S(2)}) collective-permute-start(f32[19,1,32,256]{3,2,1,0:T(8,128)S(1)} %add_add_fusion.1), channel_id=1, source_target_pairs={{4,0},{8,4},{12,8},{16,12},{20,16},{24,20},{28,24},{32,28},{36,32}... | collective-permute-start | bytes 1867784 | tf_op jit(solution)/shard_map/ppermute | solution.py:20
  55.5 4.1 %collective-permute-start.10 = (f32[19,3,1,256]{3,2,1,0:T(1,128)S(1)}, f32[19,3,1,256]{3,2,1,0:T(1,128)S(1)}, u32[]{:S(2)}, u32[]{:S(2)}) collective-permute-start(f32[19,3,1,256]{3,2,1,0:T(1,128)S(1)} %get-tuple-element.104), channel_id=1, source_target_pairs={{1,0},{2,1},{3,2},{0,3},{5,4},{6,5},{7,6},{4,7},{9,8},{10,9},{11,1... | collective-permute-start | bytes 175112 | tf_op jit(solution)/shard_map/ppermute | solution.py:20
  58.4 4.6 %collective-permute-start.11 = (f32[19,3,1,256]{3,2,1,0:T(1,128)S(1)}, f32[19,3,1,256]{3,2,1,0:T(1,128)S(1)}, u32[]{:S(2)}, u32[]{:S(2)}) collective-permute-start(f32[19,3,1,256]{3,2,1,0:T(1,128)S(1)} %get-tuple-element.103), channel_id=1, source_target_pairs={{0,1},{1,2},{2,3},{3,0},{4,5},{5,6},{6,7},{7,4},{8,9},{9,10},{10,1... | collective-permute-start | bytes 175112 | tf_op jit(solution)/shard_map/ppermute | solution.py:18
  64.2 1.8 copy-start.1
  67.0 151.6 %collective-permute-start.12 = (f32[19,1,32,256]{3,2,1,0:T(8,128)S(1)}, f32[19,1,32,256]{3,2,1,0:T(8,128)S(1)}, u32[]{:S(2)}, u32[]{:S(2)}) collective-permute-start(f32[19,1,32,256]{3,2,1,0:T(8,128)S(1)} %add_add_fusion), channel_id=1, source_target_pairs={{0,4},{4,8},{8,12},{12,16},{16,20},{20,24},{24,28},{28,32},{32,36}... | collective-permute-start | bytes 1867784 | tf_op jit(solution)/shard_map/ppermute | solution.py:18
  68.2 150.4 %collective-permute-start.13 = (f32[19,1,32,256]{3,2,1,0:T(8,128)S(1)}, f32[19,1,32,256]{3,2,1,0:T(8,128)S(1)}, u32[]{:S(2)}, u32[]{:S(2)}) collective-permute-start(f32[19,1,32,256]{3,2,1,0:T(8,128)S(1)} %add_add_fusion), channel_id=1, source_target_pairs={{4,0},{8,4},{12,8},{16,12},{20,16},{24,20},{28,24},{32,28},{36,32}... | collective-permute-start | bytes 1867784 | tf_op jit(solution)/shard_map/ppermute | solution.py:20
  218.7 3.4 %collective-permute-start.14 = (f32[19,3,1,256]{3,2,1,0:T(1,128)S(1)}, f32[19,3,1,256]{3,2,1,0:T(1,128)S(1)}, u32[]{:S(2)}, u32[]{:S(2)}) collective-permute-start(f32[19,3,1,256]{3,2,1,0:T(1,128)S(1)} %get-tuple-element.102), channel_id=1, source_target_pairs={{1,0},{2,1},{3,2},{0,3},{5,4},{6,5},{7,6},{4,7},{9,8},{10,9},{11,1... | collective-permute-start | bytes 175112 | tf_op jit(solution)/shard_map/ppermute | solution.py:20
  220.5 4.3 %collective-permute-start.15 = (f32[19,3,1,256]{3,2,1,0:T(1,128)S(1)}, f32[19,3,1,256]{3,2,1,0:T(1,128)S(1)}, u32[]{:S(2)}, u32[]{:S(2)}) collective-permute-start(f32[19,3,1,256]{3,2,1,0:T(1,128)S(1)} %get-tuple-element.101), channel_id=1, source_target_pairs={{0,1},{1,2},{2,3},{3,0},{4,5},{5,6},{6,7},{7,4},{8,9},{9,10},{10,1... | collective-permute-start | bytes 175112 | tf_op jit(solution)/shard_map/ppermute | solution.py:18
  226.0 1.1 copy-start.8
  226.0 1.3 copy-start.10
  226.1 1.4 copy-start.2
  226.1 1.6 copy-start.4
  226.1 1.8 copy-start.6
  (7 other events, 5.6 us)
